TPU v7x, 256 devices: a whole 4x4x8 slice. The times are simulated.
256 devices in a mesh: row: 16 (over z, core), col: 4 (over x), rhs: 4 (over y).
Axes of the slice: x: 4, y: 4, z: 8, core: 2. Of those that a mesh axis runs over, the one named last changes fastest.
Arguments:
- factor: bfloat16 [32768, 8192], P('row', 'col'), may hold values from -0.0625 to 0.0625
- samples: float32 [32768, 512], P('row', 'rhs'), may hold values from -6 to 6
- inverses: bfloat16 [8, 1024, 1024], P(None, 'row', 'col'), may hold values from -0.1875 to 0.1875
Outputs:
- solution: bfloat16 [8, 1024, 512], P(None, 'col', 'rhs')
- remaining: float32 [32768, 512], P(('row', 'col'), 'rhs')
All inputs are finite; a program needn't handle non-finite values.
Results may differ from a plain program's by a relative error of at most 0.006.
Values may be sent and summed in bfloat16 or wider, within the bound.
No kernel may reach another device: no remote copies, remote signals or barrier semaphores. Data moves between devices by JAX's collectives and lax.ppermute only.
A program may use at most 64 MiB of HBM per device.

v0:
```python
import jax
import jax.numpy as jnp
from jax import lax
from jax.sharding import PartitionSpec as P


def from_root(value, axis, source):
    kept = jnp.where(lax.axis_index(axis) == source, value, 0).astype(value.dtype)
    return lax.psum(kept, axis)


def shards(factor, samples, inverses):
    row_total = lax.axis_size("row")
    col_total = lax.axis_size("col")
    row_index = lax.axis_index("row")
    col_index = lax.axis_index("col")
    diag_count = inverses.shape[0]
    width = inverses.shape[1] * row_total
    part_rows = width // col_total
    row_slots = factor.shape[0] // width
    sample_cols = samples.shape[1]
    rhs_blocks = samples.reshape(row_slots, width, sample_cols)
    partial_value = jnp.zeros((row_slots, width, sample_cols), jnp.float32)
    factor_rows = jnp.arange(row_slots, dtype=jnp.int32) * row_total + row_index
    lower_mask = (
        jnp.arange(width)[:, None] >= col_index * part_rows + jnp.arange(part_rows)[None, :]
    )
    solutions = []
    for block in range(diag_count):
        owner_row = block % row_total
        slot_index = block // row_total
        inverse_cols_part = lax.all_gather(inverses[block], "row", axis=0, tiled=True)
        reduced = lax.psum_scatter(
            partial_value[slot_index], "col", scatter_dimension=0, tiled=True
        )
        own_rhs = lax.dynamic_slice_in_dim(
            rhs_blocks[slot_index], col_index * part_rows, part_rows, 0
        )
        lowered = (own_rhs - reduced).astype(jnp.bfloat16)
        inverse_part = jnp.where(lower_mask, inverse_cols_part, jnp.zeros((), jnp.bfloat16))

        def solve_term(row_start, row_count, inverse_part=inverse_part, lowered=lowered):
            return jnp.dot(inverse_part, lowered, preferred_element_type=jnp.float32)

        solved_rows = lax.psum_scatter(
            solve_term(jnp.int32(0), lax.axis_size("col") * part_rows),
            "col",
            scatter_dimension=0,
            tiled=True,
        ).astype(jnp.bfloat16)
        solved_full = lax.all_gather(solved_rows, "col", axis=0, tiled=True)
        solved_full = from_root(solved_full, "row", owner_row)
        solved_part = lax.dynamic_slice_in_dim(solved_full, col_index * part_rows, part_rows, 0)
        solutions.append(solved_part)
        col_slot = block // col_total
        column = factor[:, col_slot * width : (col_slot + 1) * width]
        keep_rows = factor_rows > block

        def apply_update(current, column=column, solved_full=solved_full, keep_rows=keep_rows):
            update = jnp.dot(column, solved_full, preferred_element_type=jnp.float32).reshape(
                row_slots, width, sample_cols
            )
            return current + jnp.where(keep_rows[:, None, None], update, jnp.float32(0.0))

        def unchanged(current):
            return current

        partial_value = lax.cond(
            col_index == block % col_total, apply_update, unchanged, partial_value
        )
    remain = lax.psum_scatter(
        partial_value.reshape(row_slots * width, sample_cols).astype(jnp.bfloat16),
        "col",
        scatter_dimension=0,
        tiled=True,
    ).astype(jnp.float32)
    out_rows = row_slots * width // col_total
    own_rows = lax.dynamic_slice_in_dim(samples, col_index * out_rows, out_rows, 0)
    return (jnp.stack(solutions), own_rows - remain)


def solution(mesh):
    in_specs = (P("row", "col"), P("row", "rhs"), P(None, "row", "col"))
    out_specs = (P(None, "col", "rhs"), P(("row", "col"), "rhs"))
    return jax.shard_map(shards, mesh=mesh, in_specs=in_specs, out_specs=out_specs, check_vma=False)
```

profile of v0, /device:TPU:8, one launch (start us, length us, event | category | flops | bytes accessed | tf_op | source)
XLA Modules:
  0.0 1471.2 jit_solution(4502672935829029276)
XLA Ops:
  8.1 21.4 %all-gather = bf16[1,1024,256]{2,1,0:T(8,128)(2,1)S(1)} all-gather(bf16[1,64,256]{2,1,0:T(8,128)(2,1)S(1)} %get-tuple-element.158), channel_id=2, replica_groups=mesh['row'=16,'col'=4,'rhs'=4] {'row'}, dimensions={1}, use_global_device_ids=true | all-gather | bytes 557056 | tf_op jit(solution)/shard_map/all_gather | solution.py:32
  31.8 22.3 %reduce-scatter.17.cloned.1.call-done = f32[256,128]{1,0:T(8,128)} async-done(((f32[1024,128]{1,0:T(8,128)}), f32[256,128]{1,0:T(8,128)}) %reduce-scatter.17.cloned.1.call-update) | async-done | bytes 131088 | tf_op jit(solution)/shard_map/reduce_scatter | solution.py:45
  55.0 12.2 all_gather.49
  68.1 5.9 fusion.64
  74.0 103.9 %all-reduce.9.cloned.1.call-done = bf16[1024,128]{1,0:T(8,128)(2,1)} async-done(((bf16[1024,128]{1,0:T(8,128)(2,1)}), bf16[1024,128]{1,0:T(8,128)(2,1)}) %all-reduce.9.cloned.1.call-update) | async-done | bytes 262160 | tf_op jit(solution)/shard_map/psum | solution.py:9
  177.9 3.6 conditional.8
  177.9 3.5 fusion.66
  182.4 16.6 %all-gather.1 = bf16[1,1024,256]{2,1,0:T(8,128)(2,1)S(1)} all-gather(bf16[1,64,256]{2,1,0:T(8,128)(2,1)S(1)} %get-tuple-element.157), channel_id=3, replica_groups=mesh['row'=16,'col'=4,'rhs'=4] {'row'}, dimensions={1}, use_global_device_ids=true | all-gather | bytes 557056 | tf_op jit(solution)/shard_map/all_gather | solution.py:32
  199.0 6.6 reduce-scatter.19.cloned.1.call-done
  207.7 25.0 %reduce-scatter.21.cloned.1.call-done = f32[256,128]{1,0:T(8,128)} async-done(((f32[1024,128]{1,0:T(8,128)}), f32[256,128]{1,0:T(8,128)}) %reduce-scatter.21.cloned.1.call-update) | async-done | bytes 131088 | tf_op jit(solution)/shard_map/reduce_scatter | solution.py:45
  233.6 12.2 all_gather.51
  246.6 109.8 %all-reduce.11.cloned.1.call-done = bf16[1024,128]{1,0:T(8,128)(2,1)} async-done(((bf16[1024,128]{1,0:T(8,128)(2,1)}), bf16[1024,128]{1,0:T(8,128)(2,1)}) %all-reduce.11.cloned.1.call-update) | async-done | bytes 262160 | tf_op jit(solution)/shard_map/psum | solution.py:9
  357.4 16.5 %all-gather.2 = bf16[1,1024,256]{2,1,0:T(8,128)(2,1)S(1)} all-gather(bf16[1,64,256]{2,1,0:T(8,128)(2,1)S(1)} %get-tuple-element.156), channel_id=4, replica_groups=mesh['row'=16,'col'=4,'rhs'=4] {'row'}, dimensions={1}, use_global_device_ids=true | all-gather | bytes 557056 | tf_op jit(solution)/shard_map/all_gather | solution.py:32
  373.9 10.6 reduce-scatter.23.cloned.1.call-done
  384.5 2.0 fusion.12
  386.6 25.0 %reduce-scatter.25.cloned.1.call-done = f32[256,128]{1,0:T(8,128)} async-done(((f32[1024,128]{1,0:T(8,128)}), f32[256,128]{1,0:T(8,128)}) %reduce-scatter.25.cloned.1.call-update) | async-done | bytes 131088 | tf_op jit(solution)/shard_map/reduce_scatter | solution.py:45
  412.5 12.2 all_gather.53
  425.5 109.9 %all-reduce.13.cloned.1.call-done = bf16[1024,128]{1,0:T(8,128)(2,1)} async-done(((bf16[1024,128]{1,0:T(8,128)(2,1)}), bf16[1024,128]{1,0:T(8,128)(2,1)}) %all-reduce.13.cloned.1.call-update) | async-done | bytes 262160 | tf_op jit(solution)/shard_map/psum | solution.py:9
  536.3 16.5 %all-gather.3 = bf16[1,1024,256]{2,1,0:T(8,128)(2,1)S(1)} all-gather(bf16[1,64,256]{2,1,0:T(8,128)(2,1)S(1)} %get-tuple-element.155), channel_id=5, replica_groups=mesh['row'=16,'col'=4,'rhs'=4] {'row'}, dimensions={1}, use_global_device_ids=true | all-gather | bytes 557056 | tf_op jit(solution)/shard_map/all_gather | solution.py:32
  552.8 12.1 reduce-scatter.27.cloned.1.call-done
  566.9 24.9 %reduce-scatter.29.cloned.1.call-done = f32[256,128]{1,0:T(8,128)} async-done(((f32[1024,128]{1,0:T(8,128)}), f32[256,128]{1,0:T(8,128)}) %reduce-scatter.29.cloned.1.call-update) | async-done | bytes 131088 | tf_op jit(solution)/shard_map/reduce_scatter | solution.py:45
  592.7 12.2 all_gather.55
  605.8 109.8 %all-reduce.15.cloned.1.call-done = bf16[1024,128]{1,0:T(8,128)(2,1)} async-done(((bf16[1024,128]{1,0:T(8,128)(2,1)}), bf16[1024,128]{1,0:T(8,128)(2,1)}) %all-reduce.15.cloned.1.call-update) | async-done | bytes 262160 | tf_op jit(solution)/shard_map/psum | solution.py:9
  716.5 16.5 %all-gather.4 = bf16[1,1024,256]{2,1,0:T(8,128)(2,1)S(1)} all-gather(bf16[1,64,256]{2,1,0:T(8,128)(2,1)S(1)} %get-tuple-element.154), channel_id=6, replica_groups=mesh['row'=16,'col'=4,'rhs'=4] {'row'}, dimensions={1}, use_global_device_ids=true | all-gather | bytes 557056 | tf_op jit(solution)/shard_map/all_gather | solution.py:32
  733.0 11.8 reduce-scatter.31.cloned.1.call-done
  744.8 2.0 fusion.16
  746.9 25.0 %reduce-scatter.33.cloned.1.call-done = f32[256,128]{1,0:T(8,128)} async-done(((f32[1024,128]{1,0:T(8,128)}), f32[256,128]{1,0:T(8,128)}) %reduce-scatter.33.cloned.1.call-update) | async-done | bytes 131088 | tf_op jit(solution)/shard_map/reduce_scatter | solution.py:45
  772.8 12.2 all_gather.57
  785.8 109.8 %all-reduce.17.cloned.1.call-done = bf16[1024,128]{1,0:T(8,128)(2,1)} async-done(((bf16[1024,128]{1,0:T(8,128)(2,1)}), bf16[1024,128]{1,0:T(8,128)(2,1)}) %all-reduce.17.cloned.1.call-update) | async-done | bytes 262160 | tf_op jit(solution)/shard_map/psum | solution.py:9
  895.7 3.8 conditional.12
  895.7 3.5 fusion.70
  900.4 16.5 %all-gather.5 = bf16[1,1024,256]{2,1,0:T(8,128)(2,1)S(1)} all-gather(bf16[1,64,256]{2,1,0:T(8,128)(2,1)S(1)} %get-tuple-element.153), channel_id=7, replica_groups=mesh['row'=16,'col'=4,'rhs'=4] {'row'}, dimensions={1}, use_global_device_ids=true | all-gather | bytes 557056 | tf_op jit(solution)/shard_map/all_gather | solution.py:32
  917.0 6.3 reduce-scatter.35.cloned.1.call-done
  925.3 24.9 %reduce-scatter.37.cloned.1.call-done = f32[256,128]{1,0:T(8,128)} async-done(((f32[1024,128]{1,0:T(8,128)}), f32[256,128]{1,0:T(8,128)}) %reduce-scatter.37.cloned.1.call-update) | async-done | bytes 131088 | tf_op jit(solution)/shard_map/reduce_scatter | solution.py:45
  951.2 12.2 all_gather.59
  964.2 109.8 %all-reduce.19.cloned.1.call-done = bf16[1024,128]{1,0:T(8,128)(2,1)} async-done(((bf16[1024,128]{1,0:T(8,128)(2,1)}), bf16[1024,128]{1,0:T(8,128)(2,1)}) %all-reduce.19.cloned.1.call-update) | async-done | bytes 262160 | tf_op jit(solution)/shard_map/psum | solution.py:9
  1074.9 16.5 %all-gather.6 = bf16[1,1024,256]{2,1,0:T(8,128)(2,1)S(1)} all-gather(bf16[1,64,256]{2,1,0:T(8,128)(2,1)S(1)} %get-tuple-element.159), channel_id=8, replica_groups=mesh['row'=16,'col'=4,'rhs'=4] {'row'}, dimensions={1}, use_global_device_ids=true | all-gather | bytes 557056 | tf_op jit(solution)/shard_map/all_gather | solution.py:32
  1091.5 10.6 reduce-scatter.39.cloned.1.call-done
  1104.1 25.0 %reduce-scatter.41.cloned.1.call-done = f32[256,128]{1,0:T(8,128)} async-done(((f32[1024,128]{1,0:T(8,128)}), f32[256,128]{1,0:T(8,128)}) %reduce-scatter.41.cloned.1.call-update) | async-done | bytes 131088 | tf_op jit(solution)/shard_map/reduce_scatter | solution.py:45
  1130.0 12.2 all_gather.61
  1143.1 109.9 %all-reduce.21.cloned.1.call-done = bf16[1024,128]{1,0:T(8,128)(2,1)} async-done(((bf16[1024,128]{1,0:T(8,128)(2,1)}), bf16[1024,128]{1,0:T(8,128)(2,1)}) %all-reduce.21.cloned.1.call-update) | async-done | bytes 262160 | tf_op jit(solution)/shard_map/psum | solution.py:9
  1253.8 16.5 %all-gather.7 = bf16[1,1024,256]{2,1,0:T(8,128)(2,1)S(1)} all-gather(bf16[1,64,256]{2,1,0:T(8,128)(2,1)S(1)} %get-tuple-element.152), channel_id=9, replica_groups=mesh['row'=16,'col'=4,'rhs'=4] {'row'}, dimensions={1}, use_global_device_ids=true | all-gather | bytes 557056 | tf_op jit(solution)/shard_map/all_gather | solution.py:32
  1270.4 12.1 reduce-scatter.43.cloned.1.call-done
  1282.4 2.0 fusion.22
  1284.5 25.0 %reduce-scatter.45.cloned.1.call-done = f32[256,128]{1,0:T(8,128)} async-done(((f32[1024,128]{1,0:T(8,128)}), f32[256,128]{1,0:T(8,128)}) %reduce-scatter.45.cloned.1.call-update) | async-done | bytes 131088 | tf_op jit(solution)/shard_map/reduce_scatter | solution.py:45
  1310.4 12.2 all_gather.63
  1323.5 109.8 %all-reduce.23.cloned.1.call-done = bf16[1024,128]{1,0:T(8,128)(2,1)} async-done(((bf16[1024,128]{1,0:T(8,128)(2,1)}), bf16[1024,128]{1,0:T(8,128)(2,1)}) %all-reduce.23.cloned.1.call-update) | async-done | bytes 262160 | tf_op jit(solution)/shard_map/psum | solution.py:9
  1441.1 21.5 %reduce-scatter.47.cloned.1.call-done = bf16[512,128]{1,0:T(8,128)(2,1)} async-done(((bf16[2048,128]{1,0:T(8,128)(2,1)}), bf16[512,128]{1,0:T(8,128)(2,1)}) %reduce-scatter.47.cloned.1.call-update) | async-done | bytes 131088 | tf_op jit(solution)/shard_map/reduce_scatter | solution.py:71
  (102 shorter events, 41.3 us)
Async XLA Ops:
  7.2 46.9 %reduce-scatter.17.cloned.1.call-start = ((), (), s32[]{:S(2)}) async-start(), calls=%async_computation.16 | async-start | bytes 655360 | tf_op jit(solution)/shard_map/reduce_scatter | solution.py:45
  31.7 146.2 %all-reduce.9.cloned.1.call-start = ((), (), s32[]{:S(2)}) async-start(), calls=%async_computation.17 | async-start | bytes 524288 | tf_op jit(solution)/shard_map/psum | solution.py:9
  68.0 137.6 %reduce-scatter.19.cloned.1.call-start = ((), (), s32[]{:S(2)}) async-start(), calls=%async_computation.18 | async-start | bytes 655360 | tf_op jit(solution)/shard_map/reduce_scatter | solution.py:33
  182.4 50.3 %reduce-scatter.21.cloned.1.call-start = ((), (), s32[]{:S(2)}) async-start(), calls=%async_computation.19 | async-start | bytes 655360 | tf_op jit(solution)/shard_map/reduce_scatter | solution.py:45
  207.7 148.8 %all-reduce.11.cloned.1.call-start = ((), (), s32[]{:S(2)}) async-start(), calls=%async_computation.20 | async-start | bytes 524288 | tf_op jit(solution)/shard_map/psum | solution.py:9
  246.6 137.9 %reduce-scatter.23.cloned.1.call-start = ((), (), s32[]{:S(2)}) async-start(), calls=%async_computation.21 | async-start | bytes 655360 | tf_op jit(solution)/shard_map/reduce_scatter | solution.py:33
  357.3 54.2 %reduce-scatter.25.cloned.1.call-start = ((), (), s32[]{:S(2)}) async-start(), calls=%async_computation.22 | async-start | bytes 655360 | tf_op jit(solution)/shard_map/reduce_scatter | solution.py:45
  386.5 148.8 %all-reduce.13.cloned.1.call-start = ((), (), s32[]{:S(2)}) async-start(), calls=%async_computation.23 | async-start | bytes 524288 | tf_op jit(solution)/shard_map/psum | solution.py:9
  425.4 139.4 %reduce-scatter.27.cloned.1.call-start = ((), (), s32[]{:S(2)}) async-start(), calls=%async_computation.24 | async-start | bytes 655360 | tf_op jit(solution)/shard_map/reduce_scatter | solution.py:33
  536.2 55.6 %reduce-scatter.29.cloned.1.call-start = ((), (), s32[]{:S(2)}) async-start(), calls=%async_computation.25 | async-start | bytes 655360 | tf_op jit(solution)/shard_map/reduce_scatter | solution.py:45
  566.9 148.7 %all-reduce.15.cloned.1.call-start = ((), (), s32[]{:S(2)}) async-start(), calls=%async_computation.26 | async-start | bytes 524288 | tf_op jit(solution)/shard_map/psum | solution.py:9
  605.7 139.1 %reduce-scatter.31.cloned.1.call-start = ((), (), s32[]{:S(2)}) async-start(), calls=%async_computation.27 | async-start | bytes 655360 | tf_op jit(solution)/shard_map/reduce_scatter | solution.py:33
  716.4 55.4 %reduce-scatter.33.cloned.1.call-start = ((), (), s32[]{:S(2)}) async-start(), calls=%async_computation.28 | async-start | bytes 655360 | tf_op jit(solution)/shard_map/reduce_scatter | solution.py:45
  746.8 148.8 %all-reduce.17.cloned.1.call-start = ((), (), s32[]{:S(2)}) async-start(), calls=%async_computation.29 | async-start | bytes 524288 | tf_op jit(solution)/shard_map/psum | solution.py:9
  785.8 137.5 %reduce-scatter.35.cloned.1.call-start = ((), (), s32[]{:S(2)}) async-start(), calls=%async_computation.30 | async-start | bytes 655360 | tf_op jit(solution)/shard_map/reduce_scatter | solution.py:33
  900.4 49.9 %reduce-scatter.37.cloned.1.call-start = ((), (), s32[]{:S(2)}) async-start(), calls=%async_computation.31 | async-start | bytes 655360 | tf_op jit(solution)/shard_map/reduce_scatter | solution.py:45
  925.3 148.8 %all-reduce.19.cloned.1.call-start = ((), (), s32[]{:S(2)}) async-start(), calls=%async_computation.32 | async-start | bytes 524288 | tf_op jit(solution)/shard_map/psum | solution.py:9
  964.2 137.9 %reduce-scatter.39.cloned.1.call-start = ((), (), s32[]{:S(2)}) async-start(), calls=%async_computation.33 | async-start | bytes 655360 | tf_op jit(solution)/shard_map/reduce_scatter | solution.py:33
  1074.9 54.2 %reduce-scatter.41.cloned.1.call-start = ((), (), s32[]{:S(2)}) async-start(), calls=%async_computation.34 | async-start | bytes 655360 | tf_op jit(solution)/shard_map/reduce_scatter | solution.py:45
  1104.0 148.9 %all-reduce.21.cloned.1.call-start = ((), (), s32[]{:S(2)}) async-start(), calls=%async_computation.35 | async-start | bytes 524288 | tf_op jit(solution)/shard_map/psum | solution.py:9
  1143.0 139.4 %reduce-scatter.43.cloned.1.call-start = ((), (), s32[]{:S(2)}) async-start(), calls=%async_computation.36 | async-start | bytes 655360 | tf_op jit(solution)/shard_map/reduce_scatter | solution.py:33
  1253.8 55.7 %reduce-scatter.45.cloned.1.call-start = ((), (), s32[]{:S(2)}) async-start(), calls=%async_computation.37 | async-start | bytes 655360 | tf_op jit(solution)/shard_map/reduce_scatter | solution.py:45
  1284.5 148.9 %all-reduce.23.cloned.1.call-start = ((), (), s32[]{:S(2)}) async-start(), calls=%async_computation.38 | async-start | bytes 524288 | tf_op jit(solution)/shard_map/psum | solution.py:9
  1323.4 139.1 %reduce-scatter.47.cloned.1.call-start = ((), (), s32[]{:S(2)}) async-start(), calls=%async_computation.39 | async-start | bytes 655360 | tf_op jit(solution)/shard_map/reduce_scatter | solution.py:71
  1441.1 23.2 %copy-start = (bf16[8,256,128]{2,1,0:T(8,128)(2,1)}, bf16[8,256,128]{2,1,0:T(8,128)(2,1)S(1)}, u32[]{:S(2)}) copy-start(bf16[8,256,128]{2,1,0:T(8,128)(2,1)S(1)} %bitcast_dynamic-update-slice_fusion) | copy-start | bytes 1572868
Sparse Core Ops, SparseCore 0:
  31.9 22.2 reduce-scatter.16
  68.1 109.7 all-reduce.8
  182.5 23.0 reduce-scatter.18
  208.6 24.0 reduce-scatter.20
  246.7 109.7 all-reduce.10
  359.4 25.0 reduce-scatter.22
  387.6 23.9 reduce-scatter.24
  425.6 109.7 all-reduce.12
  538.5 26.3 reduce-scatter.26
  567.8 23.9 reduce-scatter.28
  605.8 109.7 all-reduce.14
  718.5 26.2 reduce-scatter.30
  747.9 23.9 reduce-scatter.32
  785.9 109.7 all-reduce.16
  900.5 22.7 reduce-scatter.34
  926.2 23.9 reduce-scatter.36
  964.3 109.7 all-reduce.18
  1077.0 25.0 reduce-scatter.38
  1105.1 23.9 reduce-scatter.40
  1143.1 109.7 all-reduce.20
  1256.0 26.3 reduce-scatter.42
  1285.5 23.9 reduce-scatter.44
  1323.5 109.7 all-reduce.22
  1435.7 26.8 reduce-scatter.46
where the time goes:
time: 1470 us
  waiting for transfers between devices  1160 us (79%)
  blocking collectives  235 us (16%)
  matrix products  22.1 us (2%)
  local copies, waits for them, and re-layouts  20.6 us (1%)
  other arithmetic  16.2 us (1%)
    psum x8, waiting for transfers between devices, from_root(): return lax.psum(kept, axis)  873 us
    reduce_scatter x8, waiting for transfers between devices, shards(): lax.psum_scatter(solve_term(jnp.int32(0), lax.axis_size('col') * part_row...  197 us
    all_gather x8, blocking collectives, shards(): lax.all_gather(inverses[block], 'row', axis=0, tiled=True)  137 us
    all_gather x8, blocking collectives, shards(): solved_full = lax.all_gather(solved_rows, 'col', axis=0, tiled=True)  98 us
    reduce_scatter x7, waiting for transfers between devices, shards(): lax.psum_scatter(partial_value[slot_index], 'col', scatter_dimension=0, t...  69.9 us
  transfers between devices with their start and end apart: 24, of which 24 were waited for; matrix products, arithmetic and copies ran while one was open for 1% of the time, Pallas kernels for 0%

commit v1 on v0

--- a/solution.py
+++ b/solution.py
@@ -6,7 +6,12 @@
 
 def from_root(value, axis, source):
     kept = jnp.where(lax.axis_index(axis) == source, value, 0).astype(value.dtype)
-    return lax.psum(kept, axis)
+
+    def proceed_kinds_on_mesh(slab_in):
+        a_now = jax.lax.all_gather(slab_in, axis)
+        return jnp.sum(a_now, axis=0)
+
+    return proceed_kinds_on_mesh(kept)
 
 
 def shards(factor, samples, inverses):

time: 1470 us -> 935 us (0.64)
  waiting for transfers between devices: 1160 us -> 597 us
  other arithmetic: 16.2 us -> 40.4 us
    psum x8 -> x0, waiting for transfers between devices: 873 us -> none  [from_root(): return lax.psum(kept, axis)]
    all_gather x0 -> x8, waiting for transfers between devices: none -> 328 us  [proceed_kinds_on_mesh(): a_now = jax.lax.all_gather(slab_in, axis)]
    reduce_sum x0 -> x8, other arithmetic: none -> 24.2 us  [proceed_kinds_on_mesh(): return jnp.sum(a_now, axis=0)]
    reduce_scatter x7, waiting for transfers between devices: 69.9 us -> 47 us  [shards(): lax.psum_scatter(partial_value[slot_index], 'col', scatter_dimension=0, t...]
where the time goes in v1:
time: 935 us; the launch traced here: 934 us
  waiting for transfers between devices  597 us (64%)
  blocking collectives  243 us (26%)
  other arithmetic  40.4 us (4%)
  matrix products  22 us (2%)
  local copies, waits for them, and re-layouts  15.5 us (2%)
  between operations  14.6 us (2%)
    all_gather x8, waiting for transfers between devices, proceed_kinds_on_mesh(): a_now = jax.lax.all_gather(slab_in, axis)  328 us
    reduce_scatter x8, waiting for transfers between devices, shards(): lax.psum_scatter(solve_term(jnp.int32(0), lax.axis_size('col') * part_row...  197 us
    all_gather x8, blocking collectives, shards(): lax.all_gather(inverses[block], 'row', axis=0, tiled=True)  145 us
    all_gather x8, blocking collectives, shards(): solved_full = lax.all_gather(solved_rows, 'col', axis=0, tiled=True)  98 us
    reduce_scatter x7, waiting for transfers between devices, shards(): lax.psum_scatter(partial_value[slot_index], 'col', scatter_dimension=0, t...  47 us
    reduce_scatter x1, waiting for transfers between devices, shards(): lax.psum_scatter(partial_value.reshape(row_slots * width, sample_cols).as...  24.5 us
    reduce_sum x8, other arithmetic, proceed_kinds_on_mesh(): return jnp.sum(a_now, axis=0)  24.2 us
  transfers between devices with their start and end apart: 24, of which 24 were waited for; matrix products, arithmetic and copies ran while one was open for 1% of the time, Pallas kernels for 0%

profile of v1, /device:TPU:8, one launch (start us, length us, event | category | flops | bytes accessed | tf_op | source)
XLA Modules:
  0.0 933.7 jit_solution(4029915453405243077)
XLA Ops:
  8.1 21.4 %all-gather = bf16[1,1024,256]{2,1,0:T(8,128)(2,1)S(1)} all-gather(bf16[1,64,256]{2,1,0:T(8,128)(2,1)S(1)} %get-tuple-element.158), channel_id=2, replica_groups=mesh['row'=16,'col'=4,'rhs'=4] {'row'}, dimensions={1}, use_global_device_ids=true | all-gather | bytes 557056 | tf_op jit(solution)/shard_map/all_gather | solution.py:37
  31.8 22.3 %reduce-scatter.17.cloned.1.call-done = f32[256,128]{1,0:T(8,128)} async-done(((f32[1024,128]{1,0:T(8,128)}), f32[256,128]{1,0:T(8,128)}) %reduce-scatter.17.cloned.1.call-update) | async-done | bytes 131088 | tf_op jit(solution)/shard_map/reduce_scatter | solution.py:50
  55.0 12.2 %all_gather.97 = bf16[1024,128]{1,0:T(8,128)(2,1)S(1)} all-gather(bf16[256,128]{1,0:T(8,128)(2,1)S(1)} %convert_element_type.99), channel_id=1, replica_groups=mesh['row'=16,'col'=4,'rhs'=4] {'col'}, dimensions={0}, use_global_device_ids=true | all-gather | bytes 327680 | tf_op jit(solution)/shard_map/all_gather | solution.py:56
  68.0 5.9 fusion.64
  74.0 35.8 %all-gather.25.cloned.1.call-done = bf16[16384,128]{1,0:T(8,128)(2,1)} async-done(((bf16[1024,128]{1,0:T(8,128)(2,1)}), bf16[16384,128]{1,0:T(8,128)(2,1)}) %all-gather.25.cloned.1.call-update) | async-done | bytes 4194320 | tf_op jit(solution)/shard_map/all_gather | solution.py:11
  109.8 2.9 reduce_sum.96
  112.7 3.6 conditional.8
  112.7 3.5 fusion.66
  117.2 17.6 %all-gather.2 = bf16[1,1024,256]{2,1,0:T(8,128)(2,1)S(1)} all-gather(bf16[1,64,256]{2,1,0:T(8,128)(2,1)S(1)} %get-tuple-element.157), channel_id=4, replica_groups=mesh['row'=16,'col'=4,'rhs'=4] {'row'}, dimensions={1}, use_global_device_ids=true | all-gather | bytes 557056 | tf_op jit(solution)/shard_map/all_gather | solution.py:37
  139.6 25.0 %reduce-scatter.21.cloned.1.call-done = f32[256,128]{1,0:T(8,128)} async-done(((f32[1024,128]{1,0:T(8,128)}), f32[256,128]{1,0:T(8,128)}) %reduce-scatter.21.cloned.1.call-update) | async-done | bytes 131088 | tf_op jit(solution)/shard_map/reduce_scatter | solution.py:50
  165.5 12.2 %all_gather.101 = bf16[1024,128]{1,0:T(8,128)(2,1)S(1)} all-gather(bf16[256,128]{1,0:T(8,128)(2,1)S(1)} %convert_element_type.102), channel_id=1, replica_groups=mesh['row'=16,'col'=4,'rhs'=4] {'col'}, dimensions={0}, use_global_device_ids=true | all-gather | bytes 327680 | tf_op jit(solution)/shard_map/all_gather | solution.py:56
  178.5 41.7 %all-gather.27.cloned.1.call-done = bf16[16384,128]{1,0:T(8,128)(2,1)} async-done(((bf16[1024,128]{1,0:T(8,128)(2,1)}), bf16[16384,128]{1,0:T(8,128)(2,1)}) %all-gather.27.cloned.1.call-update) | async-done | bytes 4194320 | tf_op jit(solution)/shard_map/all_gather | solution.py:11
  220.2 2.9 reduce_sum.97
  224.0 17.6 %all-gather.4 = bf16[1,1024,256]{2,1,0:T(8,128)(2,1)S(1)} all-gather(bf16[1,64,256]{2,1,0:T(8,128)(2,1)S(1)} %get-tuple-element.156), channel_id=6, replica_groups=mesh['row'=16,'col'=4,'rhs'=4] {'row'}, dimensions={1}, use_global_device_ids=true | all-gather | bytes 557056 | tf_op jit(solution)/shard_map/all_gather | solution.py:37
  241.6 7.5 reduce-scatter.23.cloned.1.call-done
  251.2 25.0 %reduce-scatter.25.cloned.1.call-done = f32[256,128]{1,0:T(8,128)} async-done(((f32[1024,128]{1,0:T(8,128)}), f32[256,128]{1,0:T(8,128)}) %reduce-scatter.25.cloned.1.call-update) | async-done | bytes 131088 | tf_op jit(solution)/shard_map/reduce_scatter | solution.py:50
  277.1 12.2 %all_gather.105 = bf16[1024,128]{1,0:T(8,128)(2,1)S(1)} all-gather(bf16[256,128]{1,0:T(8,128)(2,1)S(1)} %convert_element_type.105), channel_id=1, replica_groups=mesh['row'=16,'col'=4,'rhs'=4] {'col'}, dimensions={0}, use_global_device_ids=true | all-gather | bytes 327680 | tf_op jit(solution)/shard_map/all_gather | solution.py:56
  290.2 41.8 %all-gather.29.cloned.1.call-done = bf16[16384,128]{1,0:T(8,128)(2,1)} async-done(((bf16[1024,128]{1,0:T(8,128)(2,1)}), bf16[16384,128]{1,0:T(8,128)(2,1)}) %all-gather.29.cloned.1.call-update) | async-done | bytes 4194320 | tf_op jit(solution)/shard_map/all_gather | solution.py:11
  335.7 17.6 %all-gather.6 = bf16[1,1024,256]{2,1,0:T(8,128)(2,1)S(1)} all-gather(bf16[1,64,256]{2,1,0:T(8,128)(2,1)S(1)} %get-tuple-element.155), channel_id=8, replica_groups=mesh['row'=16,'col'=4,'rhs'=4] {'row'}, dimensions={1}, use_global_device_ids=true | all-gather | bytes 557056 | tf_op jit(solution)/shard_map/all_gather | solution.py:37
  353.3 9.0 reduce-scatter.27.cloned.1.call-done
  364.4 24.9 %reduce-scatter.29.cloned.1.call-done = f32[256,128]{1,0:T(8,128)} async-done(((f32[1024,128]{1,0:T(8,128)}), f32[256,128]{1,0:T(8,128)}) %reduce-scatter.29.cloned.1.call-update) | async-done | bytes 131088 | tf_op jit(solution)/shard_map/reduce_scatter | solution.py:50
  390.2 12.2 %all_gather.109 = bf16[1024,128]{1,0:T(8,128)(2,1)S(1)} all-gather(bf16[256,128]{1,0:T(8,128)(2,1)S(1)} %convert_element_type.108), channel_id=1, replica_groups=mesh['row'=16,'col'=4,'rhs'=4] {'col'}, dimensions={0}, use_global_device_ids=true | all-gather | bytes 327680 | tf_op jit(solution)/shard_map/all_gather | solution.py:56
  403.2 41.8 %all-gather.31.cloned.1.call-done = bf16[16384,128]{1,0:T(8,128)(2,1)} async-done(((bf16[1024,128]{1,0:T(8,128)(2,1)}), bf16[16384,128]{1,0:T(8,128)(2,1)}) %all-gather.31.cloned.1.call-update) | async-done | bytes 4194320 | tf_op jit(solution)/shard_map/all_gather | solution.py:11
  448.8 17.8 %all-gather.8 = bf16[1,1024,256]{2,1,0:T(8,128)(2,1)S(1)} all-gather(bf16[1,64,256]{2,1,0:T(8,128)(2,1)S(1)} %get-tuple-element.154), channel_id=10, replica_groups=mesh['row'=16,'col'=4,'rhs'=4] {'row'}, dimensions={1}, use_global_device_ids=true | all-gather | bytes 557056 | tf_op jit(solution)/shard_map/all_gather | solution.py:37
  466.6 8.6 reduce-scatter.31.cloned.1.call-done
  477.2 25.0 %reduce-scatter.33.cloned.1.call-done = f32[256,128]{1,0:T(8,128)} async-done(((f32[1024,128]{1,0:T(8,128)}), f32[256,128]{1,0:T(8,128)}) %reduce-scatter.33.cloned.1.call-update) | async-done | bytes 131088 | tf_op jit(solution)/shard_map/reduce_scatter | solution.py:50
  503.1 12.2 %all_gather.113 = bf16[1024,128]{1,0:T(8,128)(2,1)S(1)} all-gather(bf16[256,128]{1,0:T(8,128)(2,1)S(1)} %convert_element_type.111), channel_id=1, replica_groups=mesh['row'=16,'col'=4,'rhs'=4] {'col'}, dimensions={0}, use_global_device_ids=true | all-gather | bytes 327680 | tf_op jit(solution)/shard_map/all_gather | solution.py:56
  516.1 41.7 %all-gather.33.cloned.1.call-done = bf16[16384,128]{1,0:T(8,128)(2,1)} async-done(((bf16[1024,128]{1,0:T(8,128)(2,1)}), bf16[16384,128]{1,0:T(8,128)(2,1)}) %all-gather.33.cloned.1.call-update) | async-done | bytes 4194320 | tf_op jit(solution)/shard_map/all_gather | solution.py:11
  557.9 2.9 reduce_sum.100
  560.7 3.8 conditional.12
  560.8 3.5 fusion.70
  565.5 17.6 %all-gather.10 = bf16[1,1024,256]{2,1,0:T(8,128)(2,1)S(1)} all-gather(bf16[1,64,256]{2,1,0:T(8,128)(2,1)S(1)} %get-tuple-element.153), channel_id=12, replica_groups=mesh['row'=16,'col'=4,'rhs'=4] {'row'}, dimensions={1}, use_global_device_ids=true | all-gather | bytes 557056 | tf_op jit(solution)/shard_map/all_gather | solution.py:37
  587.8 25.1 %reduce-scatter.37.cloned.1.call-done = f32[256,128]{1,0:T(8,128)} async-done(((f32[1024,128]{1,0:T(8,128)}), f32[256,128]{1,0:T(8,128)}) %reduce-scatter.37.cloned.1.call-update) | async-done | bytes 131088 | tf_op jit(solution)/shard_map/reduce_scatter | solution.py:50
  613.8 12.2 %all_gather.117 = bf16[1024,128]{1,0:T(8,128)(2,1)S(1)} all-gather(bf16[256,128]{1,0:T(8,128)(2,1)S(1)} %convert_element_type.113), channel_id=1, replica_groups=mesh['row'=16,'col'=4,'rhs'=4] {'col'}, dimensions={0}, use_global_device_ids=true | all-gather | bytes 327680 | tf_op jit(solution)/shard_map/all_gather | solution.py:56
  626.9 41.9 %all-gather.35.cloned.1.call-done = bf16[16384,128]{1,0:T(8,128)(2,1)} async-done(((bf16[1024,128]{1,0:T(8,128)(2,1)}), bf16[16384,128]{1,0:T(8,128)(2,1)}) %all-gather.35.cloned.1.call-update) | async-done | bytes 4194320 | tf_op jit(solution)/shard_map/all_gather | solution.py:11
  668.7 3.5 reduce_sum.101
  673.2 17.6 %all-gather.12 = bf16[1,1024,256]{2,1,0:T(8,128)(2,1)S(1)} all-gather(bf16[1,64,256]{2,1,0:T(8,128)(2,1)S(1)} %get-tuple-element.159), channel_id=14, replica_groups=mesh['row'=16,'col'=4,'rhs'=4] {'row'}, dimensions={1}, use_global_device_ids=true | all-gather | bytes 557056 | tf_op jit(solution)/shard_map/all_gather | solution.py:37
  690.8 7.5 reduce-scatter.39.cloned.1.call-done
  700.4 25.0 %reduce-scatter.41.cloned.1.call-done = f32[256,128]{1,0:T(8,128)} async-done(((f32[1024,128]{1,0:T(8,128)}), f32[256,128]{1,0:T(8,128)}) %reduce-scatter.41.cloned.1.call-update) | async-done | bytes 131088 | tf_op jit(solution)/shard_map/reduce_scatter | solution.py:50
  726.3 12.2 %all_gather.121 = bf16[1024,128]{1,0:T(8,128)(2,1)S(1)} all-gather(bf16[256,128]{1,0:T(8,128)(2,1)S(1)} %convert_element_type.115), channel_id=1, replica_groups=mesh['row'=16,'col'=4,'rhs'=4] {'col'}, dimensions={0}, use_global_device_ids=true | all-gather | bytes 327680 | tf_op jit(solution)/shard_map/all_gather | solution.py:56
  739.3 41.7 %all-gather.37.cloned.1.call-done = bf16[16384,128]{1,0:T(8,128)(2,1)} async-done(((bf16[1024,128]{1,0:T(8,128)(2,1)}), bf16[16384,128]{1,0:T(8,128)(2,1)}) %all-gather.37.cloned.1.call-update) | async-done | bytes 4194320 | tf_op jit(solution)/shard_map/all_gather | solution.py:11
  781.1 3.5 reduce_sum.102
  785.5 17.6 %all-gather.14 = bf16[1,1024,256]{2,1,0:T(8,128)(2,1)S(1)} all-gather(bf16[1,64,256]{2,1,0:T(8,128)(2,1)S(1)} %get-tuple-element.152), channel_id=16, replica_groups=mesh['row'=16,'col'=4,'rhs'=4] {'row'}, dimensions={1}, use_global_device_ids=true | all-gather | bytes 557056 | tf_op jit(solution)/shard_map/all_gather | solution.py:37
  803.1 9.0 reduce-scatter.43.cloned.1.call-done
  814.3 25.0 %reduce-scatter.45.cloned.1.call-done = f32[256,128]{1,0:T(8,128)} async-done(((f32[1024,128]{1,0:T(8,128)}), f32[256,128]{1,0:T(8,128)}) %reduce-scatter.45.cloned.1.call-update) | async-done | bytes 131088 | tf_op jit(solution)/shard_map/reduce_scatter | solution.py:50
  840.2 12.2 %all_gather.125 = bf16[1024,128]{1,0:T(8,128)(2,1)S(1)} all-gather(bf16[256,128]{1,0:T(8,128)(2,1)S(1)} %convert_element_type.117), channel_id=1, replica_groups=mesh['row'=16,'col'=4,'rhs'=4] {'col'}, dimensions={0}, use_global_device_ids=true | all-gather | bytes 327680 | tf_op jit(solution)/shard_map/all_gather | solution.py:56
  853.2 41.7 %all-gather.39.cloned.1.call-done = bf16[16384,128]{1,0:T(8,128)(2,1)} async-done(((bf16[1024,128]{1,0:T(8,128)(2,1)}), bf16[16384,128]{1,0:T(8,128)(2,1)}) %all-gather.39.cloned.1.call-update) | async-done | bytes 4194320 | tf_op jit(solution)/shard_map/all_gather | solution.py:11
  900.6 24.5 %reduce-scatter.47.cloned.1.call-done = bf16[512,128]{1,0:T(8,128)(2,1)} async-done(((bf16[2048,128]{1,0:T(8,128)(2,1)}), bf16[512,128]{1,0:T(8,128)(2,1)}) %reduce-scatter.47.cloned.1.call-update) | async-done | bytes 131088 | tf_op jit(solution)/shard_map/reduce_scatter | solution.py:76
  (110 shorter events, 56.2 us)
Async XLA Ops:
  7.2 46.9 %reduce-scatter.17.cloned.1.call-start = ((), (), s32[]{:S(2)}) async-start(), calls=%async_computation.16 | async-start | bytes 655360 | tf_op jit(solution)/shard_map/reduce_scatter | solution.py:50
  31.7 78.1 %all-gather.25.cloned.1.call-start = ((), (), s32[]{:S(2)}) async-start(), calls=%async_computation.32 | async-start | bytes 4456448 | tf_op jit(solution)/shard_map/all_gather | solution.py:11
  68.0 69.5 %reduce-scatter.19.cloned.1.call-start = ((), (), s32[]{:S(2)}) async-start(), calls=%async_computation.17 | async-start | bytes 655360 | tf_op jit(solution)/shard_map/reduce_scatter | solution.py:38
  117.2 47.4 %reduce-scatter.21.cloned.1.call-start = ((), (), s32[]{:S(2)}) async-start(), calls=%async_computation.18 | async-start | bytes 655360 | tf_op jit(solution)/shard_map/reduce_scatter | solution.py:50
  139.5 80.7 %all-gather.27.cloned.1.call-start = ((), (), s32[]{:S(2)}) async-start(), calls=%async_computation.33 | async-start | bytes 4456448 | tf_op jit(solution)/shard_map/all_gather | solution.py:11
  178.5 70.7 %reduce-scatter.23.cloned.1.call-start = ((), (), s32[]{:S(2)}) async-start(), calls=%async_computation.19 | async-start | bytes 655360 | tf_op jit(solution)/shard_map/reduce_scatter | solution.py:38
  224.0 52.2 %reduce-scatter.25.cloned.1.call-start = ((), (), s32[]{:S(2)}) async-start(), calls=%async_computation.20 | async-start | bytes 655360 | tf_op jit(solution)/shard_map/reduce_scatter | solution.py:50
  251.2 80.8 %all-gather.29.cloned.1.call-start = ((), (), s32[]{:S(2)}) async-start(), calls=%async_computation.34 | async-start | bytes 4456448 | tf_op jit(solution)/shard_map/all_gather | solution.py:11
  290.1 72.2 %reduce-scatter.27.cloned.1.call-start = ((), (), s32[]{:S(2)}) async-start(), calls=%async_computation.21 | async-start | bytes 655360 | tf_op jit(solution)/shard_map/reduce_scatter | solution.py:38
  335.7 53.6 %reduce-scatter.29.cloned.1.call-start = ((), (), s32[]{:S(2)}) async-start(), calls=%async_computation.22 | async-start | bytes 655360 | tf_op jit(solution)/shard_map/reduce_scatter | solution.py:50
  364.4 80.6 %all-gather.31.cloned.1.call-start = ((), (), s32[]{:S(2)}) async-start(), calls=%async_computation.35 | async-start | bytes 4456448 | tf_op jit(solution)/shard_map/all_gather | solution.py:11
  403.2 72.0 %reduce-scatter.31.cloned.1.call-start = ((), (), s32[]{:S(2)}) async-start(), calls=%async_computation.23 | async-start | bytes 655360 | tf_op jit(solution)/shard_map/reduce_scatter | solution.py:38
  448.7 53.5 %reduce-scatter.33.cloned.1.call-start = ((), (), s32[]{:S(2)}) async-start(), calls=%async_computation.24 | async-start | bytes 655360 | tf_op jit(solution)/shard_map/reduce_scatter | solution.py:50
  477.1 80.7 %all-gather.33.cloned.1.call-start = ((), (), s32[]{:S(2)}) async-start(), calls=%async_computation.36 | async-start | bytes 4456448 | tf_op jit(solution)/shard_map/all_gather | solution.py:11
  516.1 69.7 %reduce-scatter.35.cloned.1.call-start = ((), (), s32[]{:S(2)}) async-start(), calls=%async_computation.25 | async-start | bytes 655360 | tf_op jit(solution)/shard_map/reduce_scatter | solution.py:38
  565.4 47.5 %reduce-scatter.37.cloned.1.call-start = ((), (), s32[]{:S(2)}) async-start(), calls=%async_computation.26 | async-start | bytes 655360 | tf_op jit(solution)/shard_map/reduce_scatter | solution.py:50
  587.8 81.0 %all-gather.35.cloned.1.call-start = ((), (), s32[]{:S(2)}) async-start(), calls=%async_computation.37 | async-start | bytes 4456448 | tf_op jit(solution)/shard_map/all_gather | solution.py:11
  626.8 71.5 %reduce-scatter.39.cloned.1.call-start = ((), (), s32[]{:S(2)}) async-start(), calls=%async_computation.27 | async-start | bytes 655360 | tf_op jit(solution)/shard_map/reduce_scatter | solution.py:38
  673.1 52.3 %reduce-scatter.41.cloned.1.call-start = ((), (), s32[]{:S(2)}) async-start(), calls=%async_computation.28 | async-start | bytes 655360 | tf_op jit(solution)/shard_map/reduce_scatter | solution.py:50
  700.3 80.7 %all-gather.37.cloned.1.call-start = ((), (), s32[]{:S(2)}) async-start(), calls=%async_computation.38 | async-start | bytes 4456448 | tf_op jit(solution)/shard_map/all_gather | solution.py:11
  739.3 72.9 %reduce-scatter.43.cloned.1.call-start = ((), (), s32[]{:S(2)}) async-start(), calls=%async_computation.29 | async-start | bytes 655360 | tf_op jit(solution)/shard_map/reduce_scatter | solution.py:38
  785.5 53.8 %reduce-scatter.45.cloned.1.call-start = ((), (), s32[]{:S(2)}) async-start(), calls=%async_computation.30 | async-start | bytes 655360 | tf_op jit(solution)/shard_map/reduce_scatter | solution.py:50
  814.2 80.8 %all-gather.39.cloned.1.call-start = ((), (), s32[]{:S(2)}) async-start(), calls=%async_computation.39 | async-start | bytes 4456448 | tf_op jit(solution)/shard_map/all_gather | solution.py:11
  853.2 71.9 %reduce-scatter.47.cloned.1.call-start = ((), (), s32[]{:S(2)}) async-start(), calls=%async_computation.31 | async-start | bytes 655360 | tf_op jit(solution)/shard_map/reduce_scatter | solution.py:76
  900.6 26.2 %copy-start = (bf16[8,256,128]{2,1,0:T(8,128)(2,1)}, bf16[8,256,128]{2,1,0:T(8,128)(2,1)S(1)}, u32[]{:S(2)}) copy-start(bf16[8,256,128]{2,1,0:T(8,128)(2,1)S(1)} %bitcast_dynamic-update-slice_fusion) | copy-start | bytes 1572868
Sparse Core Ops, SparseCore 0:
  31.9 22.1 reduce-scatter.16
  68.1 41.6 all-gather.24
  117.3 20.1 reduce-scatter.18
  140.5 24.0 reduce-scatter.20
  178.6 41.6 all-gather.26
  224.1 25.0 reduce-scatter.22
  252.2 23.9 reduce-scatter.24
  290.2 41.6 all-gather.28
  335.8 26.5 reduce-scatter.26
  365.3 23.9 reduce-scatter.28
  403.3 41.6 all-gather.30
  448.8 26.2 reduce-scatter.30
  478.2 23.9 reduce-scatter.32
  516.2 41.6 all-gather.32
  565.5 20.1 reduce-scatter.34
  588.7 24.1 reduce-scatter.36
  626.9 41.7 all-gather.34
  673.2 25.0 reduce-scatter.38
  701.4 23.9 reduce-scatter.40
  739.4 41.6 all-gather.36
  785.6 26.5 reduce-scatter.42
  815.3 23.9 reduce-scatter.44
  853.3 41.6 all-gather.38
  898.9 26.2 reduce-scatter.46
